TPU v7x, 32 devices: a whole 2x2x4 slice. The times are simulated.
32 devices in a mesh: row: 4 (over z), mix: 8 (over y, x, core).
Axes of the slice: x: 2, y: 2, z: 4, core: 2. Of those that a mesh axis runs over, the one named last changes fastest.
Arguments:
- velocity: bfloat16 [64, 3, 8, 32, 128], P(None, None, 'mix', 'row'), may hold values from -6 to 6
- field_b: bfloat16 [64, 3, 8, 32, 128], P(None, None, 'mix', 'row'), may hold values from -6 to 6
- test_signs: int32 [384, 256], replicated, may hold values from 0 to 1
- row_signs: int32 [8, 32, 128], P('mix', 'row'), may hold values from 0 to 1
- sample_index: int32 [8, 4, 256], P('mix', 'row'), may hold values from 0 to 1023
Outputs:
- basis_rows: float32 [8, 4, 256, 256], P('mix', 'row')
- factor: float32 [256, 256], replicated
Inputs may be any that keep to these rules, and one draw needn't show every extreme that they name: test_signs entries are bits; the test matrix is 2 test_signs - 1. row_signs entries are bits; the sign is 2 row_signs - 1. `sample_index`: a point of the device's own block, p = x_local 128 + y; repeats may occur.
All inputs are finite; a program needn't handle non-finite values.
Results may differ from a plain program's by a relative error of at most 0.0021.
Values may be sent and summed in bfloat16 or wider, within the bound.
No kernel may reach another device: no remote copies, remote signals or barrier semaphores. Data moves between devices by JAX's collectives and lax.ppermute only.
A program may use at most 64 MiB of HBM per device.

v0:
```python
import math
import jax
import jax.numpy as jnp
from jax import lax
from jax.sharding import PartitionSpec as P


def swapped(block, axis, distance):
    count = lax.axis_size(axis)
    route = []
    for low in range(count):
        high = low | 1 << distance
        if high != low and high < count:
            route += [(low, high), (high, low)]
    return lax.ppermute(block, axis, route)


def padded(shard, sides, width):
    for axis, dim in sides:
        size, length = (lax.axis_size(axis), shard.shape[dim])
        up = [(i, (i + 1) % size) for i in range(size - 1)]
        down = [(j, i) for i, j in up]
        last = lax.slice_in_dim(shard, length - width, length, axis=dim)
        first = lax.slice_in_dim(shard, 0, width, axis=dim)
        before = lax.ppermute(last, axis, up)
        after = lax.ppermute(first, axis, down)
        shard = jnp.concatenate([before, shard, after], axis=dim)
    return shard


def curl_plane(stencil_slab):
    center = stencil_slab[:, :, 1]

    def along_x(component):
        return (center[:, component, 2:, 1:-1] - center[:, component, :-2, 1:-1]) * 0.5

    def along_y(component):
        return (center[:, component, 1:-1, 2:] - center[:, component, 1:-1, :-2]) * 0.5

    def along_z(component):
        return (
            stencil_slab[:, component, 2, 1:-1, 1:-1] - stencil_slab[:, component, 0, 1:-1, 1:-1]
        ) * 0.5

    current_x = along_y(2) - along_z(1)
    current_y = along_z(0) - along_x(2)
    current_z = along_x(1) - along_y(0)
    return jnp.stack([current_x, current_y, current_z], axis=1).astype(jnp.bfloat16)


def pair_mixing(signed, planes):
    my_index = lax.axis_index("mix")
    values = signed
    for level in range(planes.bit_length() - 1):
        partner = swapped(values, "mix", level)
        upper_bit = my_index // (1 << level) % 2
        values = jnp.where(upper_bit == 1, partner - values, values + partner)
    return values / math.sqrt(planes)


def upper_factor(gram_matrix):
    return jnp.linalg.cholesky(gram_matrix).T


def on_device(velocity, field_b, test_signs, row_signs, sample_index):
    snaps = field_b.shape[0]
    sketch_width = test_signs.shape[1]
    planes = lax.axis_size("mix")
    row_blocks = lax.axis_size("row")
    with_rims = padded(field_b, (("row", 3), ("mix", 2)), 1)
    stencil_slab = jnp.pad(with_rims.astype(jnp.float32), ((0, 0), (0, 0), (0, 0), (0, 0), (1, 1)))
    current = curl_plane(stencil_slab)
    snapshot = jnp.concatenate([velocity[:, :, 0], current], axis=1).reshape(6 * snaps, -1)
    test_matrix = (2 * test_signs - 1).astype(jnp.bfloat16)
    sketch = lax.dot_general(
        snapshot, test_matrix, (((0,), (0,)), ((), ())), preferred_element_type=jnp.float32
    ) * (1.0 / math.sqrt(6 * snaps))
    point_signs = (2 * row_signs - 1).astype(jnp.float32).reshape(-1)
    signed = sketch * point_signs[:, None]
    mixed_rows = pair_mixing(signed, planes)
    picked = jnp.take(mixed_rows, sample_index.reshape(-1), axis=0)
    picked_total = planes * row_blocks * picked.shape[0]
    local_gram = (
        jnp.dot(
            picked.T, picked, precision=lax.Precision.HIGHEST, preferred_element_type=jnp.float32
        )
        / picked_total
    )
    block_factor = upper_factor(lax.psum(local_gram, "mix"))
    every_factor = lax.all_gather(block_factor[None], "row", axis=0, tiled=True)
    stacked_gram = jnp.einsum(
        "bij,bil->jl", every_factor, every_factor, precision=lax.Precision.HIGHEST
    )
    factor = upper_factor(stacked_gram)
    solved = jax.scipy.linalg.solve_triangular(factor.T, picked.T, lower=True)
    basis_rows = solved.T.reshape(sample_index.shape + (sketch_width,))
    return (basis_rows, factor)


def solution(mesh):
    return jax.shard_map(
        on_device,
        mesh=mesh,
        in_specs=(
            P(None, None, "mix", "row", None),
            P(None, None, "mix", "row", None),
            P(),
            P("mix", "row", None),
            P("mix", "row", None),
        ),
        out_specs=(P("mix", "row", None, None), P()),
        check_vma=False,
    )
```

profile of v0, /device:TPU:0, one launch (start us, length us, event | category | flops | bytes accessed | tf_op | source)
XLA Modules:
  0.0 284.6 jit_solution(11077461579640509562)
XLA Ops:
  7.2 1.4 fusion.46
  8.6 4.9 %collective-permute-start = (bf16[64,3,1,1,128]{4,0,3,2,1:T(8,128)(2,1)S(1)}, bf16[64,3,1,1,128]{4,0,3,2,1:T(8,128)(2,1)S(1)}, u32[]{:S(2)}, u32[]{:S(2)}) collective-permute-start(bf16[64,3,1,1,128]{4,0,3,2,1:T(8,128)(2,1)S(1)} %copy.62), channel_id=1, source_target_pairs={{0,8},{8,16},{16,24},{1,9},{9,17},{17,25},{2,10},{10,18},{18,26},{... | collective-permute-start | bytes 147464 | tf_op jit(solution)/shard_map/ppermute | solution.py:25
  13.6 1.3 collective-permute-start.1
  15.3 1.1 constant_dynamic-update-slice_fusion.1
  16.4 3.2 %collective-permute-done.1 = bf16[64,3,1,1,128]{4,0,3,2,1:T(8,128)(2,1)S(1)} collective-permute-done((bf16[64,3,1,1,128]{4,0,3,2,1:T(8,128)(2,1)S(1)}, bf16[64,3,1,1,128]{4,0,3,2,1:T(8,128)(2,1)S(1)}, u32[]{:S(2)}, u32[]{:S(2)}) %collective-permute-start.1) | collective-permute-done | bytes 49184 | tf_op jit(solution)/shard_map/ppermute | solution.py:26
  19.6 1.3 collective-permute-start.3
  20.9 3.1 %collective-permute-start.2 = (bf16[64,3,1,10,128]{4,0,3,2,1:T(8,128)(2,1)S(1)}, bf16[64,3,1,10,128]{4,0,3,2,1:T(8,128)(2,1)S(1)}, u32[]{:S(2)}, u32[]{:S(2)}) collective-permute-start(bf16[64,3,1,10,128]{4,0,3,2,1:T(8,128)(2,1)S(1)} %constant_dynamic-update-slice_fusion), channel_id=1, source_target_pairs={{0,1},{1,2},{2,3},{3,4},{4,5},{5,6},{6,7},{8,9},{9,10},{10,11},{11... | collective-permute-start | bytes 1474568 | tf_op jit(solution)/shard_map/ppermute | solution.py:25
  28.0 6.6 %collective-permute-start.4 = (f32[1024,256]{1,0:T(8,128)S(1)}, f32[1024,256]{1,0:T(8,128)S(1)}, u32[]{:S(2)}, u32[]{:S(2)}) collective-permute-start(f32[1024,256]{1,0:T(8,128)S(1)} %convolution_multiply_fusion), channel_id=1, source_target_pairs={{0,1},{1,0},{2,3},{3,2},{4,5},{5,4},{6,7},{7,6},{8,9},{9,8},{10,11... | collective-permute-start | bytes 3145736 | tf_op jit(solution)/shard_map/ppermute | solution.py:15
  34.6 2.3 collective-permute-done.4
  37.0 2.8 collective-permute-start.5
  39.9 23.7 %collective-permute-done.5 = f32[1024,256]{1,0:T(8,128)S(1)} collective-permute-done((f32[1024,256]{1,0:T(8,128)S(1)}, f32[1024,256]{1,0:T(8,128)S(1)}, u32[]{:S(2)}, u32[]{:S(2)}) %collective-permute-start.5) | collective-permute-done | bytes 1048608 | tf_op jit(solution)/shard_map/ppermute | solution.py:15
  63.7 3.7 %collective-permute-start.6 = (f32[1024,256]{1,0:T(8,128)S(1)}, f32[1024,256]{1,0:T(8,128)S(1)}, u32[]{:S(2)}, u32[]{:S(2)}) collective-permute-start(f32[1024,256]{1,0:T(8,128)S(1)} %add_select_fusion), channel_id=1, source_target_pairs={{0,4},{4,0},{1,5},{5,1},{2,6},{6,2},{3,7},{7,3},{8,12},{12,8},{9,1... | collective-permute-start | bytes 3145736 | tf_op jit(solution)/shard_map/ppermute | solution.py:15
  67.5 22.6 %collective-permute-done.6 = f32[1024,256]{1,0:T(8,128)S(1)} collective-permute-done((f32[1024,256]{1,0:T(8,128)S(1)}, f32[1024,256]{1,0:T(8,128)S(1)}, u32[]{:S(2)}, u32[]{:S(2)}) %collective-permute-start.6) | collective-permute-done | bytes 1048608 | tf_op jit(solution)/shard_map/ppermute | solution.py:15
  90.2 1.0 gather_fusion
  91.3 1.1 convolution_multiply_fusion.1
  92.7 53.0 %all-reduce.4.cloned.1.call-done = f32[256,256]{0,1:T(8,128)} async-done(((f32[256,256]{0,1:T(8,128)}), f32[256,256]{0,1:T(8,128)}) %all-reduce.4.cloned.1.call-update) | async-done | bytes 262160 | tf_op jit(solution)/shard_map/psum | solution.py:89
  145.7 1.1 copy.44
  146.8 1.0 fusion.20
  147.8 11.7 %cholesky.130 = f32[128,128]{1,0:T(8,128)S(1)} custom-call(f32[128,128]{1,0:T(8,128)S(1)} %cholesky.194), custom_call_target="Cholesky" | custom-call | tf_op jit(solution)/shard_map/jit(cholesky)/cholesky | solution.py:62
  159.6 9.8 %custom-call.14 = f32[1,128,128]{1,2,0:T(8,128)S(1)} custom-call(f32[1,128,128]{2,1,0:T(8,128)S(1)} %get-tuple-element.41), custom_call_target="InvertDiagBlocksLowerTriangular" | custom-call | tf_op jit(solution)/shard_map/jit(cholesky)/cholesky | solution.py:62
  169.9 11.7 %cholesky.147 = f32[128,128]{1,0:T(8,128)S(1)} custom-call(f32[128,128]{1,0:T(8,128)S(1)} %convolution_subtract_fusion.2), custom_call_target="Cholesky" | custom-call | tf_op jit(solution)/shard_map/jit(cholesky)/cholesky | solution.py:62
  184.4 27.4 %all-gather.3.cloned.1.call-done = f32[1024,256]{0,1:T(8,128)} async-done(((f32[256,256]{0,1:T(8,128)}), f32[1024,256]{0,1:T(8,128)}) %all-gather.3.cloned.1.call-update) | async-done | bytes 1048592 | tf_op jit(solution)/shard_map/all_gather | solution.py:90
  211.8 2.6 convolution_bitcast_fusion
  214.6 11.9 %cholesky.164 = f32[128,128]{1,0:T(8,128)S(1)} custom-call(f32[128,128]{1,0:T(8,128)S(1)} %cholesky.197), custom_call_target="Cholesky" | custom-call | tf_op jit(solution)/shard_map/jit(cholesky)/cholesky | solution.py:62
  226.6 9.8 %custom-call.15 = f32[1,128,128]{1,2,0:T(8,128)S(1)} custom-call(f32[1,128,128]{2,1,0:T(8,128)S(1)} %get-tuple-element.37), custom_call_target="InvertDiagBlocksLowerTriangular" | custom-call | tf_op jit(solution)/shard_map/jit(cholesky)/cholesky | solution.py:62
  236.8 11.7 %cholesky.181 = f32[128,128]{1,0:T(8,128)S(1)} custom-call(f32[128,128]{1,0:T(8,128)S(1)} %convolution_subtract_fusion.1), custom_call_target="Cholesky" | custom-call | tf_op jit(solution)/shard_map/jit(cholesky)/cholesky | solution.py:62
  251.3 4.2 %while.1 = (s32[]{:T(128)}, f32[256,256]{1,0:T(8,128)S(1)}, s32[2,2]{1,0:T(2,128)S(1)}, f32[2,128,128]{2,1,0:T(8,128)S(1)}, s32[]{:T(128)}) while((s32[]{:T(128)}, f32[256,256]{1,0:T(8,128)S(1)}, s32[2,2]{1,0:T(2,128)S(1)}, f32[2,128,128]{2,1,0:T(8,128)S(1)}, s32[]{:T(128)}) %tuple.38), condition=%wide.while_cond, body=%wide.while_body.sunk | while | flops 2 | bytes 131189 | solution.py:95
  252.1 1.4 bitcast_dynamic-update-slice_fusion.2
  254.1 1.4 bitcast_dynamic-update-slice_fusion.2
  255.5 19.7 %custom-call.12 = f32[2,128,128]{1,2,0:T(8,128)S(1)} custom-call(f32[2,128,128]{2,1,0:T(8,128)S(1)} %get-tuple-element.10), custom_call_target="InvertDiagBlocksLowerTriangular" | custom-call | tf_op jit(solution)/shard_map/jit(_solve_triangular)/triangular_solve | solution.py:95
  276.1 0.8 copy.48
  276.9 0.8 copy.49
  (64 shorter events, 11.5 us)
Async XLA Ops:
  7.2 138.5 %all-reduce.4.cloned.1.call-start = ((), (), s32[]{:S(2)}) async-start(), calls=%async_computation | async-start | bytes 524288 | tf_op jit(solution)/shard_map/psum | solution.py:89
  8.6 6.7 %collective-permute-start = (bf16[64,3,1,1,128]{4,0,3,2,1:T(8,128)(2,1)S(1)}, bf16[64,3,1,1,128]{4,0,3,2,1:T(8,128)(2,1)S(1)}, u32[]{:S(2)}, u32[]{:S(2)}) collective-permute-start(bf16[64,3,1,1,128]{4,0,3,2,1:T(8,128)(2,1)S(1)} %copy.62), channel_id=1, source_target_pairs={{0,8},{8,16},{16,24},{1,9},{9,17},{17,25},{2,10},{10,18},{18,26},{... | collective-permute-start | bytes 147464 | tf_op jit(solution)/shard_map/ppermute | solution.py:25
  13.6 6.0 %collective-permute-start.1 = (bf16[64,3,1,1,128]{4,0,3,2,1:T(8,128)(2,1)S(1)}, bf16[64,3,1,1,128]{4,0,3,2,1:T(8,128)(2,1)S(1)}, u32[]{:S(2)}, u32[]{:S(2)}) collective-permute-start(bf16[64,3,1,1,128]{4,0,3,2,1:T(8,128)(2,1)S(1)} %copy.63), channel_id=1, source_target_pairs={{8,0},{16,8},{24,16},{9,1},{17,9},{25,17},{10,2},{18,10},{26,18},{... | collective-permute-start | bytes 147464 | tf_op jit(solution)/shard_map/ppermute | solution.py:26
  19.6 5.1 %collective-permute-start.3 = (bf16[64,3,1,10,128]{4,0,3,2,1:T(8,128)(2,1)S(1)}, bf16[64,3,1,10,128]{4,0,3,2,1:T(8,128)(2,1)S(1)}, u32[]{:S(2)}, u32[]{:S(2)}) collective-permute-start(bf16[64,3,1,10,128]{4,0,3,2,1:T(8,128)(2,1)S(1)} %constant_dynamic-update-slice_fusion), channel_id=1, source_target_pairs={{1,0},{2,1},{3,2},{4,3},{5,4},{6,5},{7,6},{9,8},{10,9},{11,10},{12... | collective-permute-start | bytes 1474568 | tf_op jit(solution)/shard_map/ppermute | solution.py:26
  20.9 4.5 %collective-permute-start.2 = (bf16[64,3,1,10,128]{4,0,3,2,1:T(8,128)(2,1)S(1)}, bf16[64,3,1,10,128]{4,0,3,2,1:T(8,128)(2,1)S(1)}, u32[]{:S(2)}, u32[]{:S(2)}) collective-permute-start(bf16[64,3,1,10,128]{4,0,3,2,1:T(8,128)(2,1)S(1)} %constant_dynamic-update-slice_fusion), channel_id=1, source_target_pairs={{0,1},{1,2},{2,3},{3,4},{4,5},{5,6},{6,7},{8,9},{9,10},{10,11},{11... | collective-permute-start | bytes 1474568 | tf_op jit(solution)/shard_map/ppermute | solution.py:25
  26.0 1.0 copy-start
  26.5 1.0 copy-start.2
  28.0 8.9 %collective-permute-start.4 = (f32[1024,256]{1,0:T(8,128)S(1)}, f32[1024,256]{1,0:T(8,128)S(1)}, u32[]{:S(2)}, u32[]{:S(2)}) collective-permute-start(f32[1024,256]{1,0:T(8,128)S(1)} %convolution_multiply_fusion), channel_id=1, source_target_pairs={{0,1},{1,0},{2,3},{3,2},{4,5},{5,4},{6,7},{7,6},{8,9},{9,8},{10,11... | collective-permute-start | bytes 3145736 | tf_op jit(solution)/shard_map/ppermute | solution.py:15
  37.0 30.4 %copy-start.1 = (s32[1,1,256]{2,1,0:T(1,128)S(1)}, s32[1,1,256]{2,1,0:T(1,128)}, u32[]{:S(2)}) copy-start(s32[1,1,256]{2,1,0:T(1,128)} %param.10) | copy-start | bytes 3076
  37.0 26.5 %collective-permute-start.5 = (f32[1024,256]{1,0:T(8,128)S(1)}, f32[1024,256]{1,0:T(8,128)S(1)}, u32[]{:S(2)}, u32[]{:S(2)}) collective-permute-start(f32[1024,256]{1,0:T(8,128)S(1)} %add_select_fusion.1), channel_id=1, source_target_pairs={{0,2},{2,0},{1,3},{3,1},{4,6},{6,4},{5,7},{7,5},{8,10},{10,8},{9,1... | collective-permute-start | bytes 3145736 | tf_op jit(solution)/shard_map/ppermute | solution.py:15
  63.7 26.4 %collective-permute-start.6 = (f32[1024,256]{1,0:T(8,128)S(1)}, f32[1024,256]{1,0:T(8,128)S(1)}, u32[]{:S(2)}, u32[]{:S(2)}) collective-permute-start(f32[1024,256]{1,0:T(8,128)S(1)} %add_select_fusion), channel_id=1, source_target_pairs={{0,4},{4,0},{1,5},{5,1},{2,6},{6,2},{3,7},{7,3},{8,12},{12,8},{9,1... | collective-permute-start | bytes 3145736 | tf_op jit(solution)/shard_map/ppermute | solution.py:15
  92.5 119.3 %all-gather.3.cloned.1.call-start = ((), (), s32[]{:S(2)}) async-start(), calls=%async_computation.1 | async-start | bytes 1310720 | tf_op jit(solution)/shard_map/all_gather | solution.py:90
Sparse Core Ops, SparseCore 0:
  92.6 53.0 all-reduce.3
  184.4 27.2 all-gather.2
where the time goes:
time: 285 us
  waiting for transfers between devices  133 us (47%)
  other arithmetic  92.6 us (32%)
  starting transfers between devices  24 us (8%)
  between operations  17 us (6%)
  local copies, waits for them, and re-layouts  11.4 us (4%)
  matrix products  5.98 us (2%)
    another operation x13, other arithmetic, upper_factor(): return jnp.linalg.cholesky(gram_matrix).T  68.8 us
    psum x1, waiting for transfers between devices, on_device(): block_factor = upper_factor(lax.psum(local_gram, 'mix'))  53 us
    ppermute x3, waiting for transfers between devices, swapped(): return lax.ppermute(block, axis, route)  48.6 us
    all_gather x1, waiting for transfers between devices, on_device(): every_factor = lax.all_gather(block_factor[None], 'row', axis=0, tiled=True)  27.4 us
    another operation x2, other arithmetic, on_device(): solved = jax.scipy.linalg.solve_triangular(factor.T, picked.T, lower=True)  19.7 us
    ppermute x3, starting transfers between devices, swapped(): return lax.ppermute(block, axis, route)  13.2 us
    ppermute x2, starting transfers between devices, padded(): before = lax.ppermute(last, axis, up)  7.99 us
  transfers between devices with their start and end apart: 9, of which 8 were waited for; matrix products, arithmetic and copies ran while one was open for 1% of the time, Pallas kernels for 0%

commit v1 on v0

--- a/solution.py
+++ b/solution.py
@@ -86,7 +86,7 @@
         )
         / picked_total
     )
-    block_factor = upper_factor(lax.psum(local_gram, "mix"))
+    block_factor = upper_factor(jnp.sum(lax.all_gather(local_gram, "mix"), axis=0))
     every_factor = lax.all_gather(block_factor[None], "row", axis=0, tiled=True)
     stacked_gram = jnp.einsum(
         "bij,bil->jl", every_factor, every_factor, precision=lax.Precision.HIGHEST

time: 285 us -> 260 us (0.912)
  waiting for transfers between devices: 133 us -> 108 us
    psum x1 -> x0, waiting for transfers between devices: 53 us -> none  [on_device(): block_factor = upper_factor(lax.psum(local_gram, 'mix'))]
    all_gather x0 -> x1, waiting for transfers between devices: none -> 27.4 us  [on_device(): lax.all_gather(local_gram, 'mix')]
where the time goes in v1:
time: 260 us; the launch traced here: 259 us
  waiting for transfers between devices  108 us (42%)
  other arithmetic  93.4 us (36%)
  starting transfers between devices  24 us (9%)
  between operations  17 us (7%)
  local copies, waits for them, and re-layouts  10.3 us (4%)
  matrix products  6 us (2%)
    another operation x13, other arithmetic, upper_factor(): return jnp.linalg.cholesky(gram_matrix).T  68.8 us
    ppermute x3, waiting for transfers between devices, swapped(): return lax.ppermute(block, axis, route)  48.6 us
    all_gather x1, waiting for transfers between devices, on_device(): every_factor = lax.all_gather(block_factor[None], 'row', axis=0, tiled=True)  28 us
    all_gather x1, waiting for transfers between devices, on_device(): lax.all_gather(local_gram, 'mix')  27.4 us
    another operation x2, other arithmetic, on_device(): solved = jax.scipy.linalg.solve_triangular(factor.T, picked.T, lower=True)  19.7 us
    ppermute x3, starting transfers between devices, swapped(): return lax.ppermute(block, axis, route)  13.2 us
    ppermute x2, starting transfers between devices, padded(): before = lax.ppermute(last, axis, up)  7.99 us
  transfers between devices with their start and end apart: 9, of which 8 were waited for; matrix products, arithmetic and copies ran while one was open for 1% of the time, Pallas kernels for 0%

profile of v1, /device:TPU:0, one launch (start us, length us, event | category | flops | bytes accessed | tf_op | source)
XLA Modules:
  0.0 259.4 jit_solution(17922887509486088498)
XLA Ops:
  7.2 1.3 fusion.46
  8.5 4.9 %collective-permute-start = (bf16[64,3,1,1,128]{4,0,3,2,1:T(8,128)(2,1)S(1)}, bf16[64,3,1,1,128]{4,0,3,2,1:T(8,128)(2,1)S(1)}, u32[]{:S(2)}, u32[]{:S(2)}) collective-permute-start(bf16[64,3,1,1,128]{4,0,3,2,1:T(8,128)(2,1)S(1)} %copy.58), channel_id=1, source_target_pairs={{0,8},{8,16},{16,24},{1,9},{9,17},{17,25},{2,10},{10,18},{18,26},{... | collective-permute-start | bytes 147464 | tf_op jit(solution)/shard_map/ppermute | solution.py:25
  13.5 1.3 collective-permute-start.1
  15.2 1.1 constant_dynamic-update-slice_fusion.1
  16.3 3.2 %collective-permute-done.1 = bf16[64,3,1,1,128]{4,0,3,2,1:T(8,128)(2,1)S(1)} collective-permute-done((bf16[64,3,1,1,128]{4,0,3,2,1:T(8,128)(2,1)S(1)}, bf16[64,3,1,1,128]{4,0,3,2,1:T(8,128)(2,1)S(1)}, u32[]{:S(2)}, u32[]{:S(2)}) %collective-permute-start.1) | collective-permute-done | bytes 49184 | tf_op jit(solution)/shard_map/ppermute | solution.py:26
  19.5 1.3 collective-permute-start.3
  20.8 3.1 %collective-permute-start.2 = (bf16[64,3,1,10,128]{4,0,3,2,1:T(8,128)(2,1)S(1)}, bf16[64,3,1,10,128]{4,0,3,2,1:T(8,128)(2,1)S(1)}, u32[]{:S(2)}, u32[]{:S(2)}) collective-permute-start(bf16[64,3,1,10,128]{4,0,3,2,1:T(8,128)(2,1)S(1)} %constant_dynamic-update-slice_fusion), channel_id=1, source_target_pairs={{0,1},{1,2},{2,3},{3,4},{4,5},{5,6},{6,7},{8,9},{9,10},{10,11},{11... | collective-permute-start | bytes 1474568 | tf_op jit(solution)/shard_map/ppermute | solution.py:25
  24.5 0.7 collective-permute-done.2
  27.9 6.6 %collective-permute-start.4 = (f32[1024,256]{1,0:T(8,128)S(1)}, f32[1024,256]{1,0:T(8,128)S(1)}, u32[]{:S(2)}, u32[]{:S(2)}) collective-permute-start(f32[1024,256]{1,0:T(8,128)S(1)} %convolution_multiply_fusion), channel_id=1, source_target_pairs={{0,1},{1,0},{2,3},{3,2},{4,5},{5,4},{6,7},{7,6},{8,9},{9,8},{10,11... | collective-permute-start | bytes 3145736 | tf_op jit(solution)/shard_map/ppermute | solution.py:15
  34.5 2.3 collective-permute-done.4
  36.9 2.8 %collective-permute-start.5 = (f32[1024,256]{1,0:T(8,128)S(1)}, f32[1024,256]{1,0:T(8,128)S(1)}, u32[]{:S(2)}, u32[]{:S(2)}) collective-permute-start(f32[1024,256]{1,0:T(8,128)S(1)} %add_select_fusion.1), channel_id=1, source_target_pairs={{0,2},{2,0},{1,3},{3,1},{4,6},{6,4},{5,7},{7,5},{8,10},{10,8},{9,1... | collective-permute-start | bytes 3145736 | tf_op jit(solution)/shard_map/ppermute | solution.py:15
  39.8 23.7 %collective-permute-done.5 = f32[1024,256]{1,0:T(8,128)S(1)} collective-permute-done((f32[1024,256]{1,0:T(8,128)S(1)}, f32[1024,256]{1,0:T(8,128)S(1)}, u32[]{:S(2)}, u32[]{:S(2)}) %collective-permute-start.5) | collective-permute-done | bytes 1048608 | tf_op jit(solution)/shard_map/ppermute | solution.py:15
  63.6 3.7 %collective-permute-start.6 = (f32[1024,256]{1,0:T(8,128)S(1)}, f32[1024,256]{1,0:T(8,128)S(1)}, u32[]{:S(2)}, u32[]{:S(2)}) collective-permute-start(f32[1024,256]{1,0:T(8,128)S(1)} %add_select_fusion), channel_id=1, source_target_pairs={{0,4},{4,0},{1,5},{5,1},{2,6},{6,2},{3,7},{7,3},{8,12},{12,8},{9,1... | collective-permute-start | bytes 3145736 | tf_op jit(solution)/shard_map/ppermute | solution.py:15
  67.4 22.6 %collective-permute-done.6 = f32[1024,256]{1,0:T(8,128)S(1)} collective-permute-done((f32[1024,256]{1,0:T(8,128)S(1)}, f32[1024,256]{1,0:T(8,128)S(1)}, u32[]{:S(2)}, u32[]{:S(2)}) %collective-permute-start.6) | collective-permute-done | bytes 1048608 | tf_op jit(solution)/shard_map/ppermute | solution.py:15
  90.1 1.0 gather_fusion
  91.2 1.1 convolution_multiply_fusion.1
  92.6 27.4 %all-gather.5.cloned.1.call-done = f32[2048,256]{1,0:T(8,128)} async-done(((f32[256,256]{1,0:T(8,128)}), f32[2048,256]{1,0:T(8,128)}) %all-gather.5.cloned.1.call-update) | async-done | bytes 2097168 | tf_op jit(solution)/shard_map/all_gather | solution.py:89
  120.0 1.8 reduce_sum.9
  121.9 11.7 %cholesky.130 = f32[128,128]{1,0:T(8,128)S(1)} custom-call(f32[128,128]{1,0:T(8,128)S(1)} %cholesky.194), custom_call_target="Cholesky" | custom-call | tf_op jit(solution)/shard_map/jit(cholesky)/cholesky | solution.py:62
  133.7 9.8 %custom-call.14 = f32[1,128,128]{1,2,0:T(8,128)S(1)} custom-call(f32[1,128,128]{2,1,0:T(8,128)S(1)} %get-tuple-element.41), custom_call_target="InvertDiagBlocksLowerTriangular" | custom-call | tf_op jit(solution)/shard_map/jit(cholesky)/cholesky | solution.py:62
  144.0 11.7 %cholesky.147 = f32[128,128]{1,0:T(8,128)S(1)} custom-call(f32[128,128]{1,0:T(8,128)S(1)} %convolution_subtract_fusion.2), custom_call_target="Cholesky" | custom-call | tf_op jit(solution)/shard_map/jit(cholesky)/cholesky | solution.py:62
  158.5 28.0 %all-gather.7.cloned.1.call-done = f32[1024,256]{0,1:T(8,128)} async-done(((f32[256,256]{0,1:T(8,128)}), f32[1024,256]{0,1:T(8,128)}) %all-gather.7.cloned.1.call-update) | async-done | bytes 1048592 | tf_op jit(solution)/shard_map/all_gather | solution.py:90
  186.6 2.6 convolution_bitcast_fusion
  189.3 11.9 %cholesky.164 = f32[128,128]{1,0:T(8,128)S(1)} custom-call(f32[128,128]{1,0:T(8,128)S(1)} %cholesky.197), custom_call_target="Cholesky" | custom-call | tf_op jit(solution)/shard_map/jit(cholesky)/cholesky | solution.py:62
  201.3 9.8 %custom-call.15 = f32[1,128,128]{1,2,0:T(8,128)S(1)} custom-call(f32[1,128,128]{2,1,0:T(8,128)S(1)} %get-tuple-element.37), custom_call_target="InvertDiagBlocksLowerTriangular" | custom-call | tf_op jit(solution)/shard_map/jit(cholesky)/cholesky | solution.py:62
  211.6 11.7 %cholesky.181 = f32[128,128]{1,0:T(8,128)S(1)} custom-call(f32[128,128]{1,0:T(8,128)S(1)} %convolution_subtract_fusion.1), custom_call_target="Cholesky" | custom-call | tf_op jit(solution)/shard_map/jit(cholesky)/cholesky | solution.py:62
  226.0 4.2 %while.1 = (s32[]{:T(128)}, f32[256,256]{1,0:T(8,128)S(1)}, s32[2,2]{1,0:T(2,128)S(1)}, f32[2,128,128]{2,1,0:T(8,128)S(1)}, s32[]{:T(128)}) while((s32[]{:T(128)}, f32[256,256]{1,0:T(8,128)S(1)}, s32[2,2]{1,0:T(2,128)S(1)}, f32[2,128,128]{2,1,0:T(8,128)S(1)}, s32[]{:T(128)}) %tuple.38), condition=%wide.while_cond, body=%wide.while_body.sunk | while | flops 2 | bytes 131189 | solution.py:95
  226.9 1.4 bitcast_dynamic-update-slice_fusion.2
  228.8 1.4 bitcast_dynamic-update-slice_fusion.2
  230.2 19.7 %custom-call.12 = f32[2,128,128]{1,2,0:T(8,128)S(1)} custom-call(f32[2,128,128]{2,1,0:T(8,128)S(1)} %get-tuple-element.10), custom_call_target="InvertDiagBlocksLowerTriangular" | custom-call | tf_op jit(solution)/shard_map/jit(_solve_triangular)/triangular_solve | solution.py:95
  250.8 0.8 copy.45
  251.7 0.8 copy.46
  (65 shorter events, 10.9 us)
Async XLA Ops:
  7.2 112.8 %all-gather.5.cloned.1.call-start = ((), (), s32[]{:S(2)}) async-start(), calls=%async_computation | async-start | bytes 2359296 | tf_op jit(solution)/shard_map/all_gather | solution.py:89
  8.5 6.7 %collective-permute-start = (bf16[64,3,1,1,128]{4,0,3,2,1:T(8,128)(2,1)S(1)}, bf16[64,3,1,1,128]{4,0,3,2,1:T(8,128)(2,1)S(1)}, u32[]{:S(2)}, u32[]{:S(2)}) collective-permute-start(bf16[64,3,1,1,128]{4,0,3,2,1:T(8,128)(2,1)S(1)} %copy.58), channel_id=1, source_target_pairs={{0,8},{8,16},{16,24},{1,9},{9,17},{17,25},{2,10},{10,18},{18,26},{... | collective-permute-start | bytes 147464 | tf_op jit(solution)/shard_map/ppermute | solution.py:25
  13.5 6.0 %collective-permute-start.1 = (bf16[64,3,1,1,128]{4,0,3,2,1:T(8,128)(2,1)S(1)}, bf16[64,3,1,1,128]{4,0,3,2,1:T(8,128)(2,1)S(1)}, u32[]{:S(2)}, u32[]{:S(2)}) collective-permute-start(bf16[64,3,1,1,128]{4,0,3,2,1:T(8,128)(2,1)S(1)} %copy.59), channel_id=1, source_target_pairs={{8,0},{16,8},{24,16},{9,1},{17,9},{25,17},{10,2},{18,10},{26,18},{... | collective-permute-start | bytes 147464 | tf_op jit(solution)/shard_map/ppermute | solution.py:26
  19.5 5.1 %collective-permute-start.3 = (bf16[64,3,1,10,128]{4,0,3,2,1:T(8,128)(2,1)S(1)}, bf16[64,3,1,10,128]{4,0,3,2,1:T(8,128)(2,1)S(1)}, u32[]{:S(2)}, u32[]{:S(2)}) collective-permute-start(bf16[64,3,1,10,128]{4,0,3,2,1:T(8,128)(2,1)S(1)} %constant_dynamic-update-slice_fusion), channel_id=1, source_target_pairs={{1,0},{2,1},{3,2},{4,3},{5,4},{6,5},{7,6},{9,8},{10,9},{11,10},{12... | collective-permute-start | bytes 1474568 | tf_op jit(solution)/shard_map/ppermute | solution.py:26
  20.8 4.5 %collective-permute-start.2 = (bf16[64,3,1,10,128]{4,0,3,2,1:T(8,128)(2,1)S(1)}, bf16[64,3,1,10,128]{4,0,3,2,1:T(8,128)(2,1)S(1)}, u32[]{:S(2)}, u32[]{:S(2)}) collective-permute-start(bf16[64,3,1,10,128]{4,0,3,2,1:T(8,128)(2,1)S(1)} %constant_dynamic-update-slice_fusion), channel_id=1, source_target_pairs={{0,1},{1,2},{2,3},{3,4},{4,5},{5,6},{6,7},{8,9},{9,10},{10,11},{11... | collective-permute-start | bytes 1474568 | tf_op jit(solution)/shard_map/ppermute | solution.py:25
  25.9 1.0 copy-start
  26.4 1.0 copy-start.2
  27.9 8.9 %collective-permute-start.4 = (f32[1024,256]{1,0:T(8,128)S(1)}, f32[1024,256]{1,0:T(8,128)S(1)}, u32[]{:S(2)}, u32[]{:S(2)}) collective-permute-start(f32[1024,256]{1,0:T(8,128)S(1)} %convolution_multiply_fusion), channel_id=1, source_target_pairs={{0,1},{1,0},{2,3},{3,2},{4,5},{5,4},{6,7},{7,6},{8,9},{9,8},{10,11... | collective-permute-start | bytes 3145736 | tf_op jit(solution)/shard_map/ppermute | solution.py:15
  36.9 30.4 %copy-start.1 = (s32[1,1,256]{2,1,0:T(1,128)S(1)}, s32[1,1,256]{2,1,0:T(1,128)}, u32[]{:S(2)}) copy-start(s32[1,1,256]{2,1,0:T(1,128)} %param.10) | copy-start | bytes 3076
  36.9 26.5 %collective-permute-start.5 = (f32[1024,256]{1,0:T(8,128)S(1)}, f32[1024,256]{1,0:T(8,128)S(1)}, u32[]{:S(2)}, u32[]{:S(2)}) collective-permute-start(f32[1024,256]{1,0:T(8,128)S(1)} %add_select_fusion.1), channel_id=1, source_target_pairs={{0,2},{2,0},{1,3},{3,1},{4,6},{6,4},{5,7},{7,5},{8,10},{10,8},{9,1... | collective-permute-start | bytes 3145736 | tf_op jit(solution)/shard_map/ppermute | solution.py:15
  63.6 26.4 %collective-permute-start.6 = (f32[1024,256]{1,0:T(8,128)S(1)}, f32[1024,256]{1,0:T(8,128)S(1)}, u32[]{:S(2)}, u32[]{:S(2)}) collective-permute-start(f32[1024,256]{1,0:T(8,128)S(1)} %add_select_fusion), channel_id=1, source_target_pairs={{0,4},{4,0},{1,5},{5,1},{2,6},{6,2},{3,7},{7,3},{8,12},{12,8},{9,1... | collective-permute-start | bytes 3145736 | tf_op jit(solution)/shard_map/ppermute | solution.py:15
  92.4 94.2 %all-gather.7.cloned.1.call-start = ((), (), s32[]{:S(2)}) async-start(), calls=%async_computation.1 | async-start | bytes 1310720 | tf_op jit(solution)/shard_map/all_gather | solution.py:90
Sparse Core Ops, SparseCore 0:
  92.5 27.4 all-gather.4
  158.6 27.9 all-gather.6
